TPU v7x, 32 devices: a whole 2x2x4 slice. The times are simulated.
32 devices in a mesh: grp: 4 (over z), inner: 8 (over y, x, core).
Axes of the slice: x: 2, y: 2, z: 4, core: 2. Of those that a mesh axis runs over, the one named last changes fastest.
Arguments:
- design: float32 [8, 4096, 1024], P('inner', 'grp'), may hold values from -6 to 6
- row_signs: int32 [8, 4096], P('inner', 'grp'), may hold values from 0 to 1
- kept_rows: int32 [8, 2048], P('inner'), may hold values from 0 to 4095, as said below
Outputs:
- factored: float32 [2048, 1024], P('grp')
Inputs may be any that keep to these rules, and one draw needn't show every extreme that they name: `kept_rows`: within each block the 2048 kept row numbers are distinct, and each block keeps its first and its last row.
All inputs are finite; a program needn't handle non-finite values.
Results may differ from a plain program's by a relative error of at most 0.0048.
Values may be sent and summed in bfloat16 or wider, within the bound.
No kernel may reach another device: no remote copies, remote signals or barrier semaphores. Data moves between devices by JAX's collectives and lax.ppermute only.
A program may use at most 64 MiB of HBM per device.

v0:
```python
import math
import jax
import jax.numpy as jnp
from jax import lax
from jax.sharding import PartitionSpec as P

COLS_DONE = 8
epsilon = 1e-06


def sign_table(row_ids, col_ids):
    common_bits = jnp.bitwise_and(row_ids[:, None], col_ids[None, :])
    ones_total = jnp.zeros(common_bits.shape, jnp.int32)
    for bit_pos in range(4):
        ones_total = ones_total + jnp.bitwise_and(jnp.right_shift(common_bits, bit_pos), 1)
    return 1.0 - 2.0 * jnp.bitwise_and(ones_total, 1).astype(jnp.float32)


def pick_rows(table_rows, chosen_rows):
    return jnp.take(table_rows, chosen_rows, axis=0)


def on_device(design, row_signs, kept_rows):
    block_count, local_rows, columns = design.shape
    keep_count = kept_rows.shape[1]
    groups = lax.axis_size("grp")
    owned_rows = keep_count // groups
    highest = lax.Precision.HIGHEST
    sixteen = jnp.arange(16, dtype=jnp.int32)
    hadamard = sign_table(sixteen, sixteen).astype(jnp.bfloat16)
    flipped = (design * (1 - 2 * row_signs).astype(jnp.float32)[:, :, None]).astype(jnp.bfloat16)
    lowest = flipped.reshape(block_count * local_rows // 16, 16, columns)
    first_pass = jnp.einsum(
        "hc,ncd->nhd", hadamard, lowest, preferred_element_type=jnp.float32
    ).astype(jnp.bfloat16)
    middle_view = first_pass.reshape(block_count * local_rows // 256, 16, 16, columns)
    second_pass = jnp.einsum(
        "hb,mbcd->mhcd", hadamard, middle_view, preferred_element_type=jnp.float32
    ).astype(jnp.bfloat16)
    second_pass = second_pass.reshape(block_count, local_rows, columns)
    gathered_rows = lax.all_to_all(second_pass, "grp", split_axis=2, concat_axis=1, tiled=True)
    col_count = gathered_rows.shape[2]
    by_piece = gathered_rows.reshape(block_count, 16, 256, col_count)
    mixed_rows = jnp.einsum("ha,nakd->nhkd", hadamard, by_piece, preferred_element_type=jnp.float32)
    mixed_rows = mixed_rows.reshape(block_count, 16 * 256, col_count)
    picked = jax.vmap(pick_rows)(mixed_rows, kept_rows)
    partial_value = jnp.sum(picked, axis=0)
    summed = lax.psum(partial_value, "inner")
    sketch = lax.all_to_all(summed, "grp", split_axis=0, concat_axis=1, tiled=True)
    sketch = sketch * (1.0 / (64.0 * math.sqrt(keep_count)))
    row_base = lax.axis_index("grp") * owned_rows
    global_rows = row_base + jnp.arange(owned_rows, dtype=jnp.int32)

    def reflect(col_index, current):
        column = jnp.where(global_rows >= col_index, current[:, col_index], 0.0)
        is_pivot = (global_rows == col_index).astype(jnp.float32)
        norm_sq, crossed, pivot_row = lax.psum(
            (
                jnp.sum(column * column),
                jnp.dot(column, current, precision=highest),
                jnp.dot(is_pivot, current, precision=highest),
            ),
            "grp",
        )
        pivot_value = pivot_row[col_index]
        head_value = -jnp.where(pivot_value >= 0, 1.0, -1.0) * jnp.sqrt(norm_sq)
        length = 2.0 * (norm_sq - head_value * pivot_value) + epsilon
        projected_row = crossed - head_value * pivot_row
        vector = column - head_value * is_pivot
        return current - vector[:, None] * (2.0 * projected_row / length)[None, :]

    result = lax.fori_loop(0, COLS_DONE, reflect, sketch)
    return result


def solution(mesh):
    return jax.shard_map(
        on_device,
        mesh=mesh,
        in_specs=(P("inner", "grp", None), P("inner", "grp"), P("inner", None)),
        out_specs=P("grp", None),
        check_vma=False,
    )
```

profile of v0, /device:TPU:0, one launch (start us, length us, event | category | flops | bytes accessed | tf_op | source)
XLA Modules:
  0.0 397.2 jit_solution(10092679646443896874)
XLA Ops:
  7.2 2.5 multiply_convert_fusion
  13.1 7.7 %copy.22 = bf16[1,1024,1024]{1,0,2:T(2,128)(2,1)} copy(bf16[1,1024,1024]{2,1,0:T(8,128)(2,1)S(1)} %bitcast.77) | data formatting | bytes 4194304 | tf_op jit(solution)/shard_map/reshape | solution.py:40
  21.4 12.8 %reduce.2 = bf16[1024,1024]{1,0:T(8,128)(2,1)S(1)} reduce(bf16[1024,1,1024]{2,1,0:T(2,128)(2,1)} %bitcast.75, bf16[]{:T(256)} %broadcast.106), dimensions={1}, to_apply=%bitcast.43.reduce_sub_computation | reduce | bytes 4194306
  34.2 2.8 reshape.93
  36.9 6.5 %all-to-all-start = ((bf16[4,2,131072]{2,1,0:T(2,128)(2,1)}), bf16[4,2,131072]{2,1,0:T(2,128)(2,1)S(1)}, u32[]{:S(2)}, u32[]{:S(2)}) async-start(bf16[4,2,131072]{2,1,0:T(2,128)(2,1)} %reshape.93), calls=%async_computation | async-start | bytes 4194304 | tf_op jit(solution)/shard_map/all_to_all | solution.py:41
  43.5 48.1 %all-to-all-done = bf16[4,2,131072]{2,1,0:T(2,128)(2,1)S(1)} async-done(((bf16[4,2,131072]{2,1,0:T(2,128)(2,1)}), bf16[4,2,131072]{2,1,0:T(2,128)(2,1)S(1)}, u32[]{:S(2)}, u32[]{:S(2)}) %all-to-all-start) | async-done | bytes 2097184 | tf_op jit(solution)/shard_map/all_to_all | solution.py:41
  91.6 3.4 reshape.94
  94.9 3.0 copy.29
  97.9 2.6 copy.23
  100.5 2.9 convolution_bitcast_fusion
  103.4 4.4 %copy.25 = f32[1,16,256,256]{3,2,1,0:T(8,128)} copy(f32[1,16,256,256]{3,1,2,0:T(8,128)S(1)} %convolution_bitcast_fusion) | data formatting | bytes 8388608 | tf_op jit(solution)/shard_map/ha,nakd->nhkd/transpose | solution.py:44
  107.8 21.4 %gather_fusion = f32[2048,256]{1,0:T(8,128)S(1)} fusion(f32[1,4096,256]{2,1,0:T(8,128)} %bitcast.74, s32[2048]{0:T(1024)S(1)} %bitcast.73), kind=kCustom, calls=%fused_computation | custom fusion | bytes 4210688 | tf_op jit(solution)/shard_map/vmap(jit(_take))/gather | solution.py:20
  130.8 61.1 %all-reduce.5.cloned.1.call-done = f32[4,512,256]{2,1,0:T(8,128)} async-done(((f32[4,512,256]{2,1,0:T(8,128)}), f32[4,512,256]{2,1,0:T(8,128)}) %all-reduce.5.cloned.1.call-update) | async-done | bytes 2097168 | tf_op jit(solution)/shard_map/psum | solution.py:48
  191.9 4.5 %all-to-all-start.1 = ((f32[4,512,256]{2,1,0:T(8,128)}), f32[4,512,256]{2,1,0:T(8,128)S(1)}, u32[]{:S(2)}, u32[]{:S(2)}) async-start(f32[4,512,256]{2,1,0:T(8,128)} %all-reduce.5.cloned.1.call-done), calls=%async_computation.1 | async-start | bytes 4194304 | tf_op jit(solution)/shard_map/all_to_all | solution.py:49
  196.4 47.1 %all-to-all-done.1 = f32[4,512,256]{2,1,0:T(8,128)S(1)} async-done(((f32[4,512,256]{2,1,0:T(8,128)}), f32[4,512,256]{2,1,0:T(8,128)S(1)}, u32[]{:S(2)}, u32[]{:S(2)}) %all-to-all-start.1) | async-done | bytes 2097184 | tf_op jit(solution)/shard_map/all_to_all | solution.py:49
  245.1 1.9 copy.26
  247.0 141.5 %while.14 = (s32[]{:T(128)}, f32[512,1024]{0,1:T(8,128)S(1)}, s32[]{:T(128)}, s32[]{:T(128)}, f32[]{:T(128)}, /*index=5*/f32[]{:T(128)}, f32[]{:T(128)}, f32[]{:T(128)}, f32[]{:T(128)}) while((s32[]{:T(128)}, f32[512,1024]{0,1:T(8,128)S(1)}, s32[]{:T(128)}, s32[]{:T(128)}, f32[]{:T(128)}, /*index=5*/f32[]{:T(128)}, f32[]{:T(128)}, ...), condition=%wide.region_6.7_spmd.clone, body=%wide.region_1.6_spmd.clone.sunk | while | flops 13643786 | bytes 8453379 | solution.py:72
  247.6 1.8 fusion.55
  250.5 10.8 %all-reduce.2 = (f32[1024]{0:T(1024)S(1)}, f32[1024]{0:T(1024)S(1)}, f32[]{:T(128)}) all-reduce(f32[1024]{0:T(1024)S(1)} %bitcast.83, f32[1024]{0:T(1024)S(1)} %bitcast.84, f32[]{:T(128)} %get-tuple-element.117), channel_id=1, replica_groups=mesh['grp'=4,'inner'=8] {'grp'}, use_global_device_ids=true, to_apply=%region_5.5 | all-reduce | flops 2049 | bytes 16392 | tf_op jit(solution)/shard_map/while/body/eval_jaxpr/psum | solution.py:57
  268.7 9.9 %all-reduce.2 = (f32[1024]{0:T(1024)S(1)}, f32[1024]{0:T(1024)S(1)}, f32[]{:T(128)}) all-reduce(f32[1024]{0:T(1024)S(1)} %bitcast.83, f32[1024]{0:T(1024)S(1)} %bitcast.84, f32[]{:T(128)} %get-tuple-element.117), channel_id=1, replica_groups=mesh['grp'=4,'inner'=8] {'grp'}, use_global_device_ids=true, to_apply=%region_5.5 | all-reduce | flops 2049 | bytes 16392 | tf_op jit(solution)/shard_map/while/body/eval_jaxpr/psum | solution.py:57
  285.9 10.8 %all-reduce.2 = (f32[1024]{0:T(1024)S(1)}, f32[1024]{0:T(1024)S(1)}, f32[]{:T(128)}) all-reduce(f32[1024]{0:T(1024)S(1)} %bitcast.83, f32[1024]{0:T(1024)S(1)} %bitcast.84, f32[]{:T(128)} %get-tuple-element.117), channel_id=1, replica_groups=mesh['grp'=4,'inner'=8] {'grp'}, use_global_device_ids=true, to_apply=%region_5.5 | all-reduce | flops 2049 | bytes 16392 | tf_op jit(solution)/shard_map/while/body/eval_jaxpr/psum | solution.py:57
  301.1 1.8 fusion.55
  304.0 9.9 %all-reduce.2 = (f32[1024]{0:T(1024)S(1)}, f32[1024]{0:T(1024)S(1)}, f32[]{:T(128)}) all-reduce(f32[1024]{0:T(1024)S(1)} %bitcast.83, f32[1024]{0:T(1024)S(1)} %bitcast.84, f32[]{:T(128)} %get-tuple-element.117), channel_id=1, replica_groups=mesh['grp'=4,'inner'=8] {'grp'}, use_global_device_ids=true, to_apply=%region_5.5 | all-reduce | flops 2049 | bytes 16392 | tf_op jit(solution)/shard_map/while/body/eval_jaxpr/psum | solution.py:57
  318.4 1.8 fusion.55
  321.3 10.8 %all-reduce.2 = (f32[1024]{0:T(1024)S(1)}, f32[1024]{0:T(1024)S(1)}, f32[]{:T(128)}) all-reduce(f32[1024]{0:T(1024)S(1)} %bitcast.83, f32[1024]{0:T(1024)S(1)} %bitcast.84, f32[]{:T(128)} %get-tuple-element.117), channel_id=1, replica_groups=mesh['grp'=4,'inner'=8] {'grp'}, use_global_device_ids=true, to_apply=%region_5.5 | all-reduce | flops 2049 | bytes 16392 | tf_op jit(solution)/shard_map/while/body/eval_jaxpr/psum | solution.py:57
  336.5 1.8 fusion.55
  339.4 9.9 %all-reduce.2 = (f32[1024]{0:T(1024)S(1)}, f32[1024]{0:T(1024)S(1)}, f32[]{:T(128)}) all-reduce(f32[1024]{0:T(1024)S(1)} %bitcast.83, f32[1024]{0:T(1024)S(1)} %bitcast.84, f32[]{:T(128)} %get-tuple-element.117), channel_id=1, replica_groups=mesh['grp'=4,'inner'=8] {'grp'}, use_global_device_ids=true, to_apply=%region_5.5 | all-reduce | flops 2049 | bytes 16392 | tf_op jit(solution)/shard_map/while/body/eval_jaxpr/psum | solution.py:57
  353.8 1.8 fusion.55
  356.7 10.8 %all-reduce.2 = (f32[1024]{0:T(1024)S(1)}, f32[1024]{0:T(1024)S(1)}, f32[]{:T(128)}) all-reduce(f32[1024]{0:T(1024)S(1)} %bitcast.83, f32[1024]{0:T(1024)S(1)} %bitcast.84, f32[]{:T(128)} %get-tuple-element.117), channel_id=1, replica_groups=mesh['grp'=4,'inner'=8] {'grp'}, use_global_device_ids=true, to_apply=%region_5.5 | all-reduce | flops 2049 | bytes 16392 | tf_op jit(solution)/shard_map/while/body/eval_jaxpr/psum | solution.py:57
  371.9 1.8 fusion.55
  374.8 9.9 %all-reduce.2 = (f32[1024]{0:T(1024)S(1)}, f32[1024]{0:T(1024)S(1)}, f32[]{:T(128)}) all-reduce(f32[1024]{0:T(1024)S(1)} %bitcast.83, f32[1024]{0:T(1024)S(1)} %bitcast.84, f32[]{:T(128)} %get-tuple-element.117), channel_id=1, replica_groups=mesh['grp'=4,'inner'=8] {'grp'}, use_global_device_ids=true, to_apply=%region_5.5 | all-reduce | flops 2049 | bytes 16392 | tf_op jit(solution)/shard_map/while/body/eval_jaxpr/psum | solution.py:57
  388.5 1.8 copy.27
  (97 shorter events, 33.5 us)
Async XLA Ops:
  36.9 6.5 %copy-start = (s32[1,2048]{1,0:T(1,128)S(1)}, s32[1,2048]{1,0:T(1,128)}, u32[]{:S(2)}) copy-start(s32[1,2048]{1,0:T(1,128)} %param.7) | copy-start | bytes 24580
  36.9 54.7 %all-to-all-start = ((bf16[4,2,131072]{2,1,0:T(2,128)(2,1)}), bf16[4,2,131072]{2,1,0:T(2,128)(2,1)S(1)}, u32[]{:S(2)}, u32[]{:S(2)}) async-start(bf16[4,2,131072]{2,1,0:T(2,128)(2,1)} %reshape.93), calls=%async_computation | async-start | bytes 4194304 | tf_op jit(solution)/shard_map/all_to_all | solution.py:41
  43.4 148.5 %all-reduce.5.cloned.1.call-start = ((), (), s32[]{:S(2)}) async-start(), calls=%async_computation.2 | async-start | bytes 4194304 | tf_op jit(solution)/shard_map/psum | solution.py:48
  191.9 51.6 %all-to-all-start.1 = ((f32[4,512,256]{2,1,0:T(8,128)}), f32[4,512,256]{2,1,0:T(8,128)S(1)}, u32[]{:S(2)}, u32[]{:S(2)}) async-start(f32[4,512,256]{2,1,0:T(8,128)} %all-reduce.5.cloned.1.call-done), calls=%async_computation.1 | async-start | bytes 4194304 | tf_op jit(solution)/shard_map/all_to_all | solution.py:49
Sparse Core Ops, SparseCore 0:
  131.0 60.9 all-reduce.4
where the time goes:
time: 398 us; the launch traced here: 397 us
  waiting for transfers between devices  156 us (39%)
  blocking collectives  82.7 us (21%)
  local copies, waits for them, and re-layouts  56 us (14%)
  matrix products  28 us (7%)
  other arithmetic  27.4 us (7%)
  loops' own time  22.4 us (6%)
  between operations  13.5 us (3%)
  starting transfers between devices  11 us (3%)
    psum x8, blocking collectives, reflect(): lax.psum((jnp.sum(column * column), jnp.dot(column, current, precision=hi...  82.7 us
    psum x1, waiting for transfers between devices, on_device(): summed = lax.psum(partial_value, 'inner')  61.1 us
    all_to_all x1, waiting for transfers between devices, on_device(): lax.all_to_all(second_pass, 'grp', split_axis=2, concat_axis=1, tiled=True)  48.1 us
    all_to_all x1, waiting for transfers between devices, on_device(): lax.all_to_all(summed, 'grp', split_axis=0, concat_axis=1, tiled=True)  47.1 us
    another operation x1, loops' own time, on_device(): result = lax.fori_loop(0, COLS_DONE, reflect, sketch)  22.4 us
    gather x2, local copies, waits for them, and re-layouts, pick_rows(): return jnp.take(table_rows, chosen_rows, axis=0)  21.4 us
    dot_general x8, matrix products, reflect(): jnp.dot(column, current, precision=highest)  14.5 us
    unnamed x1, other arithmetic  12.8 us
  transfers between devices with their start and end apart: 3, of which 3 were waited for; matrix products, arithmetic and copies ran while one was open for 0% of the time, Pallas kernels for 0%

commit v1 on v0

--- a/solution.py
+++ b/solution.py
@@ -38,7 +38,10 @@
         "hb,mbcd->mhcd", hadamard, middle_view, preferred_element_type=jnp.float32
     ).astype(jnp.bfloat16)
     second_pass = second_pass.reshape(block_count, local_rows, columns)
-    gathered_rows = lax.all_to_all(second_pass, "grp", split_axis=2, concat_axis=1, tiled=True)
+    size = lax.axis_size("grp")
+    shards = jnp.stack(jnp.split(second_pass, size, axis=2), axis=0)
+    shards = lax.all_to_all(shards, "grp", split_axis=0, concat_axis=0)
+    gathered_rows = jnp.concatenate(shards, axis=1)
     col_count = gathered_rows.shape[2]
     by_piece = gathered_rows.reshape(block_count, 16, 256, col_count)
     mixed_rows = jnp.einsum("ha,nakd->nhkd", hadamard, by_piece, preferred_element_type=jnp.float32)

time: 398 us -> 363 us (0.912)
  local copies, waits for them, and re-layouts: 56 us -> 35.5 us
  other arithmetic: 27.4 us -> 16.2 us
    unnamed x1 -> x0, other arithmetic: 12.8 us -> none
    unnamed x6 -> x2, local copies, waits for them, and re-layouts: 9.63 us -> 0.01 us
    reshape x1 -> x0, local copies, waits for them, and re-layouts: 7.75 us -> none  [on_device(): second_pass = second_pass.reshape(block_count, local_rows, columns)]
where the time goes in v1:
time: 363 us; the launch traced here: 362 us
  waiting for transfers between devices  156 us (43%)
  blocking collectives  82.8 us (23%)
  local copies, waits for them, and re-layouts  35.5 us (10%)
  matrix products  26.4 us (7%)
  loops' own time  20.3 us (6%)
  other arithmetic  16.2 us (4%)
  between operations  13.5 us (4%)
  starting transfers between devices  11 us (3%)
    psum x8, blocking collectives, reflect(): lax.psum((jnp.sum(column * column), jnp.dot(column, current, precision=hi...  82.8 us
    psum x1, waiting for transfers between devices, on_device(): summed = lax.psum(partial_value, 'inner')  61 us
    all_to_all x1, waiting for transfers between devices, on_device(): shards = lax.all_to_all(shards, 'grp', split_axis=0, concat_axis=0)  48.1 us
    all_to_all x1, waiting for transfers between devices, on_device(): lax.all_to_all(summed, 'grp', split_axis=0, concat_axis=1, tiled=True)  47.1 us
    gather x2, local copies, waits for them, and re-layouts, pick_rows(): return jnp.take(table_rows, chosen_rows, axis=0)  21.4 us
    another operation x1, loops' own time, on_device(): result = lax.fori_loop(0, COLS_DONE, reflect, sketch)  20.3 us
    dot_general x8, matrix products, reflect(): jnp.dot(column, current, precision=highest)  14.5 us
    dot_general x8, matrix products, reflect(): jnp.dot(is_pivot, current, precision=highest)  8.36 us
  transfers between devices with their start and end apart: 3, of which 3 were waited for; matrix products, arithmetic and copies ran while one was open for 0% of the time, Pallas kernels for 0%

profile of v1, /device:TPU:0, one launch (start us, length us, event | category | flops | bytes accessed | tf_op | source)
XLA Modules:
  0.0 361.9 jit_solution(16937396548421528979)
XLA Ops:
  7.2 2.5 multiply_convert_fusion
  10.4 1.5 convert_bitcast_fusion
  13.3 1.6 pad_maximum_fusion
  14.8 6.5 %all-to-all-start = ((bf16[4,1,1024,256]{3,2,1,0:T(8,128)(2,1)}), bf16[4,1,1024,256]{3,2,1,0:T(8,128)(2,1)S(1)}, u32[]{:S(2)}, u32[]{:S(2)}) async-start(bf16[4,1,1024,256]{3,2,1,0:T(8,128)(2,1)} %pad_maximum_fusion), calls=%async_computation | async-start | bytes 4194304 | tf_op jit(solution)/shard_map/all_to_all | solution.py:43
  21.4 48.1 %all-to-all-done = bf16[4,1,1024,256]{3,2,1,0:T(8,128)(2,1)S(1)} async-done(((bf16[4,1,1024,256]{3,2,1,0:T(8,128)(2,1)}), bf16[4,1,1024,256]{3,2,1,0:T(8,128)(2,1)S(1)}, u32[]{:S(2)}, u32[]{:S(2)}) %all-to-all-start) | async-done | bytes 2097184 | tf_op jit(solution)/shard_map/all_to_all | solution.py:43
  69.5 1.3 convolution_bitcast_fusion
  70.9 4.4 %copy.9 = f32[1,16,256,256]{3,2,1,0:T(8,128)} copy(f32[1,16,256,256]{3,1,2,0:T(8,128)S(1)} %convolution_bitcast_fusion) | data formatting | bytes 8388608 | tf_op jit(solution)/shard_map/ha,nakd->nhkd/transpose | solution.py:47
  75.2 21.4 %gather_fusion = f32[2048,256]{1,0:T(8,128)S(1)} fusion(f32[1,4096,256]{2,1,0:T(8,128)} %bitcast.77, s32[2048]{0:T(1024)S(1)} %bitcast.76), kind=kCustom, calls=%fused_computation | custom fusion | bytes 4210688 | tf_op jit(solution)/shard_map/vmap(jit(_take))/gather | solution.py:20
  96.6 1.7 broadcast_select_fusion.2
  98.3 61.0 %all-reduce.5.cloned.1.call-done = f32[4,512,256]{2,1,0:T(8,128)} async-done(((f32[4,512,256]{2,1,0:T(8,128)}), f32[4,512,256]{2,1,0:T(8,128)}) %all-reduce.5.cloned.1.call-update) | async-done | bytes 2097168 | tf_op jit(solution)/shard_map/psum | solution.py:51
  159.3 4.5 %all-to-all-start.1 = ((f32[4,512,256]{2,1,0:T(8,128)}), f32[4,512,256]{2,1,0:T(8,128)S(1)}, u32[]{:S(2)}, u32[]{:S(2)}) async-start(f32[4,512,256]{2,1,0:T(8,128)} %all-reduce.5.cloned.1.call-done), calls=%async_computation.1 | async-start | bytes 4194304 | tf_op jit(solution)/shard_map/all_to_all | solution.py:52
  163.8 47.1 %all-to-all-done.1 = f32[4,512,256]{2,1,0:T(8,128)S(1)} async-done(((f32[4,512,256]{2,1,0:T(8,128)}), f32[4,512,256]{2,1,0:T(8,128)S(1)}, u32[]{:S(2)}, u32[]{:S(2)}) %all-to-all-start.1) | async-done | bytes 2097184 | tf_op jit(solution)/shard_map/all_to_all | solution.py:52
  211.0 1.5 multiply_bitcast_fusion
  212.5 1.9 copy.10
  214.4 138.8 %while.14 = (s32[]{:T(128)}, f32[512,1024]{0,1:T(8,128)S(1)}, s32[]{:T(128)}, s32[]{:T(128)}, f32[]{:T(128)}, /*index=5*/f32[]{:T(128)}, f32[]{:T(128)}, f32[]{:T(128)}, f32[]{:T(128)}) while((s32[]{:T(128)}, f32[512,1024]{0,1:T(8,128)S(1)}, s32[]{:T(128)}, s32[]{:T(128)}, f32[]{:T(128)}, /*index=5*/f32[]{:T(128)}, f32[]{:T(128)}, ...), condition=%wide.region_6.7_spmd.clone, body=%wide.region_1.6_spmd.clone.sunk | while | flops 13643786 | bytes 8453379 | solution.py:75
  215.0 1.8 fusion.55
  217.9 10.8 %all-reduce.2 = (f32[1024]{0:T(1024)S(1)}, f32[1024]{0:T(1024)S(1)}, f32[]{:T(128)}) all-reduce(f32[1024]{0:T(1024)S(1)} %bitcast.83, f32[1024]{0:T(1024)S(1)} %bitcast.84, f32[]{:T(128)} %get-tuple-element.121), channel_id=1, replica_groups=mesh['grp'=4,'inner'=8] {'grp'}, use_global_device_ids=true, to_apply=%region_5.5 | all-reduce | flops 2049 | bytes 16392 | tf_op jit(solution)/shard_map/while/body/eval_jaxpr/psum | solution.py:60
  232.8 1.8 fusion.55
  235.7 9.9 %all-reduce.2 = (f32[1024]{0:T(1024)S(1)}, f32[1024]{0:T(1024)S(1)}, f32[]{:T(128)}) all-reduce(f32[1024]{0:T(1024)S(1)} %bitcast.83, f32[1024]{0:T(1024)S(1)} %bitcast.84, f32[]{:T(128)} %get-tuple-element.121), channel_id=1, replica_groups=mesh['grp'=4,'inner'=8] {'grp'}, use_global_device_ids=true, to_apply=%region_5.5 | all-reduce | flops 2049 | bytes 16392 | tf_op jit(solution)/shard_map/while/body/eval_jaxpr/psum | solution.py:60
  249.7 1.8 fusion.55
  252.6 10.8 %all-reduce.2 = (f32[1024]{0:T(1024)S(1)}, f32[1024]{0:T(1024)S(1)}, f32[]{:T(128)}) all-reduce(f32[1024]{0:T(1024)S(1)} %bitcast.83, f32[1024]{0:T(1024)S(1)} %bitcast.84, f32[]{:T(128)} %get-tuple-element.121), channel_id=1, replica_groups=mesh['grp'=4,'inner'=8] {'grp'}, use_global_device_ids=true, to_apply=%region_5.5 | all-reduce | flops 2049 | bytes 16392 | tf_op jit(solution)/shard_map/while/body/eval_jaxpr/psum | solution.py:60
  267.5 1.8 fusion.55
  270.4 9.9 %all-reduce.2 = (f32[1024]{0:T(1024)S(1)}, f32[1024]{0:T(1024)S(1)}, f32[]{:T(128)}) all-reduce(f32[1024]{0:T(1024)S(1)} %bitcast.83, f32[1024]{0:T(1024)S(1)} %bitcast.84, f32[]{:T(128)} %get-tuple-element.121), channel_id=1, replica_groups=mesh['grp'=4,'inner'=8] {'grp'}, use_global_device_ids=true, to_apply=%region_5.5 | all-reduce | flops 2049 | bytes 16392 | tf_op jit(solution)/shard_map/while/body/eval_jaxpr/psum | solution.py:60
  284.4 1.8 fusion.55
  287.3 10.8 %all-reduce.2 = (f32[1024]{0:T(1024)S(1)}, f32[1024]{0:T(1024)S(1)}, f32[]{:T(128)}) all-reduce(f32[1024]{0:T(1024)S(1)} %bitcast.83, f32[1024]{0:T(1024)S(1)} %bitcast.84, f32[]{:T(128)} %get-tuple-element.121), channel_id=1, replica_groups=mesh['grp'=4,'inner'=8] {'grp'}, use_global_device_ids=true, to_apply=%region_5.5 | all-reduce | flops 2049 | bytes 16392 | tf_op jit(solution)/shard_map/while/body/eval_jaxpr/psum | solution.py:60
  302.2 1.8 fusion.55
  305.1 9.9 %all-reduce.2 = (f32[1024]{0:T(1024)S(1)}, f32[1024]{0:T(1024)S(1)}, f32[]{:T(128)}) all-reduce(f32[1024]{0:T(1024)S(1)} %bitcast.83, f32[1024]{0:T(1024)S(1)} %bitcast.84, f32[]{:T(128)} %get-tuple-element.121), channel_id=1, replica_groups=mesh['grp'=4,'inner'=8] {'grp'}, use_global_device_ids=true, to_apply=%region_5.5 | all-reduce | flops 2049 | bytes 16392 | tf_op jit(solution)/shard_map/while/body/eval_jaxpr/psum | solution.py:60
  319.1 1.8 fusion.55
  322.0 10.8 %all-reduce.2 = (f32[1024]{0:T(1024)S(1)}, f32[1024]{0:T(1024)S(1)}, f32[]{:T(128)}) all-reduce(f32[1024]{0:T(1024)S(1)} %bitcast.83, f32[1024]{0:T(1024)S(1)} %bitcast.84, f32[]{:T(128)} %get-tuple-element.121), channel_id=1, replica_groups=mesh['grp'=4,'inner'=8] {'grp'}, use_global_device_ids=true, to_apply=%region_5.5 | all-reduce | flops 2049 | bytes 16392 | tf_op jit(solution)/shard_map/while/body/eval_jaxpr/psum | solution.py:60
  336.9 1.8 fusion.55
  339.8 9.9 %all-reduce.2 = (f32[1024]{0:T(1024)S(1)}, f32[1024]{0:T(1024)S(1)}, f32[]{:T(128)}) all-reduce(f32[1024]{0:T(1024)S(1)} %bitcast.83, f32[1024]{0:T(1024)S(1)} %bitcast.84, f32[]{:T(128)} %get-tuple-element.121), channel_id=1, replica_groups=mesh['grp'=4,'inner'=8] {'grp'}, use_global_device_ids=true, to_apply=%region_5.5 | all-reduce | flops 2049 | bytes 16392 | tf_op jit(solution)/shard_map/while/body/eval_jaxpr/psum | solution.py:60
  353.3 1.8 copy.11
  (92 shorter events, 24.1 us)
Async XLA Ops:
  14.8 6.5 %copy-start = (s32[1,2048]{1,0:T(1,128)S(1)}, s32[1,2048]{1,0:T(1,128)}, u32[]{:S(2)}) copy-start(s32[1,2048]{1,0:T(1,128)} %param.7) | copy-start | bytes 24580
  14.8 54.7 %all-to-all-start = ((bf16[4,1,1024,256]{3,2,1,0:T(8,128)(2,1)}), bf16[4,1,1024,256]{3,2,1,0:T(8,128)(2,1)S(1)}, u32[]{:S(2)}, u32[]{:S(2)}) async-start(bf16[4,1,1024,256]{3,2,1,0:T(8,128)(2,1)} %pad_maximum_fusion), calls=%async_computation | async-start | bytes 4194304 | tf_op jit(solution)/shard_map/all_to_all | solution.py:43
  21.3 138.0 %all-reduce.5.cloned.1.call-start = ((), (), s32[]{:S(2)}) async-start(), calls=%async_computation.2 | async-start | bytes 4194304 | tf_op jit(solution)/shard_map/psum | solution.py:51
  159.3 51.6 %all-to-all-start.1 = ((f32[4,512,256]{2,1,0:T(8,128)}), f32[4,512,256]{2,1,0:T(8,128)S(1)}, u32[]{:S(2)}, u32[]{:S(2)}) async-start(f32[4,512,256]{2,1,0:T(8,128)} %all-reduce.5.cloned.1.call-done), calls=%async_computation.1 | async-start | bytes 4194304 | tf_op jit(solution)/shard_map/all_to_all | solution.py:52
Sparse Core Ops, SparseCore 0:
  98.4 60.8 all-reduce.4
